TPU v7x, 32 devices: a whole 2x2x4 slice. The times are simulated.
32 devices in a mesh: mem: 2 (over x), col: 16 (over z, y, core).
Axes of the slice: x: 2, y: 2, z: 4, core: 2. Of those that a mesh axis runs over, the one named last changes fastest.
Arguments:
- perturbations: bfloat16 [2, 16, 384, 768], P('mem', None, 'col'), may hold values from -6 to 6
- gradient: float32 [16, 384, 768], P(None, 'col'), may hold values from -6 to 6
- member_weights: float32 [2], P('mem'), may hold values from 0.5 to 2
- scale_weights: float32 [3], replicated, may hold values from 0.2 to 2
- lon_filter: bfloat16 [3, 768, 768], P(None, 'mem'), may hold values from -1 to 1.5
- lat_filter: bfloat16 [3, 384, 384], P(None, 'col'), may hold values from -1 to 1.5
Outputs:
- increment: float32 [16, 384, 768], P('mem', 'col')
All inputs are finite; a program needn't handle non-finite values.
Results may differ from a plain program's by a relative error of at most 0.01.
Values may be sent and summed in bfloat16 or wider, within the bound.
A program may use at most 64 MiB of HBM per device.

v0:
```python
import jax
import jax.numpy as jnp
from jax import lax
from jax.sharding import PartitionSpec as P


def on_device(perturbations, gradient, member_weights, scale_weights, lon_filter, lat_filter):
    member = perturbations[0].astype(jnp.float32)
    schur = (member * gradient).astype(jnp.bfloat16)
    levels = lax.all_to_all(schur, "col", split_axis=0, concat_axis=1, tiled=True)
    along = jnp.einsum(
        "laj,sij->lsai",
        levels,
        lax.all_gather(lon_filter, "mem", axis=1, tiled=True),
        preferred_element_type=jnp.float32,
    ).astype(jnp.bfloat16)
    across = jnp.einsum(
        "sab,lsbi->lsai",
        lax.all_gather(lat_filter, "col", axis=1, tiled=True),
        along,
        preferred_element_type=jnp.float32,
    )
    filtered = jnp.einsum("s,lsai->lai", scale_weights, across).astype(jnp.bfloat16)
    back = lax.all_to_all(filtered, "col", split_axis=1, concat_axis=0, tiled=True)
    terms = member_weights[0] * member * back.astype(jnp.float32)
    return lax.psum_scatter(terms, "mem", scatter_dimension=0, tiled=True)


def solution(mesh):
    placed = (
        P("mem", None, "col", None),
        P(None, "col", None),
        P("mem"),
        P(),
        P(None, "mem", None),
        P(None, "col", None),
    )
    return jax.shard_map(
        on_device, mesh=mesh, in_specs=placed, out_specs=P("mem", "col", None), check_vma=False
    )
```

profile of v0, /device:TPU:0, one launch (start us, length us, event | category | flops | bytes accessed | tf_op | source)
XLA Modules:
  0.0 129.6 jit_solution(12170853550535788724)
XLA Ops:
  6.5 0.7 all-gather.2.cloned.1.call-update
  7.3 0.4 copy-done.1
  7.6 0.4 copy-done.2
  8.0 0.9 fusion.5
  8.9 7.4 %all-to-all-start = ((bf16[16,24,768]{2,1,0:T(8,128)(2,1)}), bf16[16,24,768]{2,1,0:T(8,128)(2,1)S(1)}, u32[]{:S(2)}, u32[]{:S(2)}) async-start(bf16[16,24,768]{2,1,0:T(8,128)(2,1)} %fusion.5), calls=%async_computation | async-start | bytes 1179648 | tf_op jit(solution)/shard_map/all_to_all | solution.py:10
  16.4 29.1 %all_gather.7 = bf16[3,384,384]{2,1,0:T(8,128)(2,1)S(1)} all-gather(bf16[3,24,384]{2,1,0:T(8,128)(2,1)S(1)} %copy-done.3), channel_id=1, replica_groups=mesh['mem'=2,'col'=16] {'col'}, dimensions={1}, use_global_device_ids=true | all-gather | bytes 940032 | tf_op jit(solution)/shard_map/all_gather | solution.py:19
  45.5 0.0 all-to-all-done
  45.5 15.5 %all-gather.2.cloned.1.call-done = bf16[3,768,768]{2,1,0:T(8,128)(2,1)} async-done(((bf16[3,384,768]{2,1,0:T(8,128)(2,1)}), bf16[3,768,768]{2,1,0:T(8,128)(2,1)}) %all-gather.2.cloned.1.call-update) | async-done | bytes 3538960 | tf_op jit(solution)/shard_map/all_gather | solution.py:14
  61.0 5.9 %convolution_bitcast_fusion = bf16[3,384,768]{1,2,0:T(8,128)(2,1)} fusion(bf16[3,384,384]{2,1,0:T(8,128)(2,1)S(1)} %all_gather.7, bf16[384,768,1]{1,0,2:T(8,128)(2,1)S(1)} %bitcast.56, bf16[3,768,768]{2,1,0:T(8,128)(2,1)} %all-gather.2.cloned.1.call-done), kind=kOutput, calls=%fused_computation | convolution fusion | flops 2039316480 | bytes 6782976 | tf_op jit(solution)/shard_map/sab,lsbi->lsai/dot_general | solution.py:17
  66.9 4.0 %copy.12 = bf16[3,384,768]{2,0,1:T(4,128)(2,1)S(1)} copy(bf16[3,384,768]{1,2,0:T(8,128)(2,1)} %convolution_bitcast_fusion) | data formatting | bytes 3538944 | tf_op jit(solution)/shard_map/reshape.6
  70.9 1.4 %fusion.10 = bf16[1,384,768]{2,0,1:T(2,128)(2,1)S(1)} fusion(bf16[3,384,768]{2,0,1:T(4,128)(2,1)S(1)} %copy.12, f32[3]{0:T(128)S(1)} %copy-done), kind=kOutput, calls=%fused_computation.13 | convolution fusion | flops 1769472 | bytes 2359308 | tf_op jit(solution)/shard_map/s,lsai->lai/dot_general | solution.py:23
  72.2 0.1 copy.19
  72.3 0.9 copy.20
  73.2 0.5 broadcast
  73.8 4.4 %reduce = bf16[384,768]{1,0:T(8,128)(2,1)S(1)} reduce(bf16[384,1,768]{2,1,0:T(2,128)(2,1)S(1)} %bitcast.54, bf16[]{:T(256)} %broadcast), dimensions={1}, to_apply=%bitcast.51.reduce_sub_computation | reduce | bytes 1179650
  78.1 1.0 reshape.33
  79.1 5.6 %all-to-all-start.1 = ((bf16[16,2,9216]{2,1,0:T(2,128)(2,1)}), bf16[16,2,9216]{2,1,0:T(2,128)(2,1)S(1)}, u32[]{:S(2)}, u32[]{:S(2)}) async-start(bf16[16,2,9216]{2,1,0:T(2,128)(2,1)} %reshape.33), calls=%async_computation.1 | async-start | bytes 1179648 | tf_op jit(solution)/shard_map/all_to_all | solution.py:24
  84.7 0.0 reduce-scatter.2.cloned.1.call-start
  85.4 14.7 %all-to-all-done.1 = bf16[16,2,9216]{2,1,0:T(2,128)(2,1)S(1)} async-done(((bf16[16,2,9216]{2,1,0:T(2,128)(2,1)}), bf16[16,2,9216]{2,1,0:T(2,128)(2,1)S(1)}, u32[]{:S(2)}, u32[]{:S(2)}) %all-to-all-start.1) | async-done | bytes 589856 | tf_op jit(solution)/shard_map/all_to_all | solution.py:24
  100.1 0.5 reshape.34
  100.6 0.1 copy.14
  100.7 1.2 fusion.4
  101.8 0.0 reduce-scatter.2.cloned.1.call-update
  101.9 20.9 %reduce-scatter.2.cloned.1.call-done = f32[8,24,768]{2,1,0:T(8,128)} async-done(((f32[16,24,768]{2,1,0:T(8,128)}), f32[8,24,768]{2,1,0:T(8,128)}) %reduce-scatter.2.cloned.1.call-update) | async-done | bytes 589840 | tf_op jit(solution)/shard_map/reduce_scatter | solution.py:26
  (7 shorter events, 0.0 us)
Async XLA Ops:
  6.5 64.3 %copy-start = (f32[3]{0:T(128)S(1)}, f32[3]{0:T(128)}, u32[]{:S(2)}) copy-start(f32[3]{0:T(128)} %param.9) | copy-start | bytes 40
  6.5 1.1 copy-start.1
  6.5 1.5 %copy-start.2 = (f32[16,24,768]{2,1,0:T(8,128)S(1)}, f32[16,24,768]{2,1,0:T(8,128)}, u32[]{:S(2)}) copy-start(f32[16,24,768]{2,1,0:T(8,128)} %param.7) | copy-start | bytes 3538948
  6.5 54.4 %all-gather.2.cloned.1.call-start = ((), (), s32[]{:S(2)}) async-start(), calls=%async_computation.3 | async-start | bytes 5308416 | tf_op jit(solution)/shard_map/all_gather | solution.py:14
  8.0 8.4 %copy-start.3 = (bf16[3,24,384]{2,1,0:T(8,128)(2,1)S(1)}, bf16[3,24,384]{2,1,0:T(8,128)(2,1)}, u32[]{:S(2)}) copy-start(bf16[3,24,384]{2,1,0:T(8,128)(2,1)} %param.11) | copy-start | bytes 165892
  8.9 36.5 %all-to-all-start = ((bf16[16,24,768]{2,1,0:T(8,128)(2,1)}), bf16[16,24,768]{2,1,0:T(8,128)(2,1)S(1)}, u32[]{:S(2)}, u32[]{:S(2)}) async-start(bf16[16,24,768]{2,1,0:T(8,128)(2,1)} %fusion.5), calls=%async_computation | async-start | bytes 1179648 | tf_op jit(solution)/shard_map/all_to_all | solution.py:10
  79.1 21.0 %all-to-all-start.1 = ((bf16[16,2,9216]{2,1,0:T(2,128)(2,1)}), bf16[16,2,9216]{2,1,0:T(2,128)(2,1)S(1)}, u32[]{:S(2)}, u32[]{:S(2)}) async-start(bf16[16,2,9216]{2,1,0:T(2,128)(2,1)} %reshape.33), calls=%async_computation.1 | async-start | bytes 1179648 | tf_op jit(solution)/shard_map/all_to_all | solution.py:24
  84.7 38.0 %reduce-scatter.2.cloned.1.call-start = ((), (), s32[]{:S(2)}) async-start(), calls=%async_computation.4 | async-start | bytes 1769472 | tf_op jit(solution)/shard_map/reduce_scatter | solution.py:26
Sparse Core Ops, SparseCore 0:
  8.9 52.0 all-gather.1
  102.0 20.7 reduce-scatter.1
where the time goes:
time: 130 us
  waiting for transfers between devices  51.8 us (40%)
  blocking collectives  29.1 us (22%)
  between operations  14.1 us (11%)
  starting transfers between devices  13.1 us (10%)
  local copies, waits for them, and re-layouts  7.76 us (6%)
  matrix products  7.27 us (6%)
  other arithmetic  6.47 us (5%)
    all_gather x1, blocking collectives, on_device(): lax.all_gather(lat_filter, 'col', axis=1, tiled=True)  29.1 us
    reduce_scatter x1, waiting for transfers between devices, on_device(): return lax.psum_scatter(terms, 'mem', scatter_dimension=0, tiled=True)  20.9 us
    all_gather x1, waiting for transfers between devices, on_device(): lax.all_gather(lon_filter, 'mem', axis=1, tiled=True)  15.5 us
    all_to_all x1, waiting for transfers between devices, on_device(): lax.all_to_all(filtered, 'col', split_axis=1, concat_axis=0, tiled=True)  14.7 us
    all_to_all x1, starting transfers between devices, on_device(): lax.all_to_all(schur, 'col', split_axis=0, concat_axis=1, tiled=True)  7.41 us
    dot_general x1, matrix products, on_device(): jnp.einsum('sab,lsbi->lsai', lax.all_gather(lat_filter, 'col', axis=1, ti...  5.91 us
    all_to_all x1, starting transfers between devices, on_device(): lax.all_to_all(filtered, 'col', split_axis=1, concat_axis=0, tiled=True)  5.62 us
    unnamed x1, other arithmetic  4.37 us
  transfers between devices with their start and end apart: 4, of which 3 were waited for; matrix products, arithmetic and copies ran while one was open for 1% of the time, Pallas kernels for 0%

commit v1 on v0

--- a/solution.py
+++ b/solution.py
@@ -4,15 +4,33 @@
 from jax.sharding import PartitionSpec as P
 
 
+def work_around(x, axis, dim, make, out_dim):
+    ways, here, step = (lax.axis_size(axis), lax.axis_index(axis), x.shape[dim])
+    results = []
+    for far in range(ways):
+        arriving = (
+            lax.ppermute(x, axis, [(d, (d + 1) % ways) for d in range(ways)])
+            if far + 1 < ways
+            else x
+        )
+        results.append(make(x, (here - far) % ways * step))
+        x = arriving
+    line = jnp.concatenate(results[::-1], axis=out_dim)
+    return jnp.roll(line, (here + 1) * results[0].shape[out_dim], axis=out_dim)
+
+
 def on_device(perturbations, gradient, member_weights, scale_weights, lon_filter, lat_filter):
     member = perturbations[0].astype(jnp.float32)
     schur = (member * gradient).astype(jnp.bfloat16)
     levels = lax.all_to_all(schur, "col", split_axis=0, concat_axis=1, tiled=True)
-    along = jnp.einsum(
-        "laj,sij->lsai",
-        levels,
-        lax.all_gather(lon_filter, "mem", axis=1, tiled=True),
-        preferred_element_type=jnp.float32,
+    along = work_around(
+        lon_filter,
+        "mem",
+        1,
+        lambda part, at: jnp.einsum(
+            "laj,sij->lsai", levels, part, preferred_element_type=jnp.float32
+        ),
+        3,
     ).astype(jnp.bfloat16)
     across = jnp.einsum(
         "sab,lsbi->lsai",

time: 130 us -> 120 us (0.923)
  waiting for transfers between devices: 51.8 us -> 36.9 us
  matrix products: 7.27 us -> 9.75 us
  starting transfers between devices: 13.1 us -> 15.1 us
  other arithmetic: 6.47 us -> 7.86 us
    all_gather x1 -> x0, waiting for transfers between devices: 15.5 us -> none  [on_device(): lax.all_gather(lon_filter, 'mem', axis=1, tiled=True)]
    dot_general x0 -> x2, matrix products: none -> 3.69 us  [on_device(): jnp.einsum('laj,sij->lsai', levels, part, preferred_element_type=jnp.floa...]
    ppermute x0 -> x1, starting transfers between devices: none -> 2.97 us  [work_around(): lax.ppermute(x, axis, [(d, (d + 1) % ways) for d in range(ways)])]
    all_to_all x1, starting transfers between devices: 7.41 us -> 5.94 us  [on_device(): lax.all_to_all(schur, 'col', split_axis=0, concat_axis=1, tiled=True)]
    convert_element_type x1, other arithmetic: 0.94 us -> 2.35 us  [on_device(): schur = (member * gradient).astype(jnp.bfloat16)]
  transfers between devices with their start and end apart: 4 -> 4, of which waited for: 3 -> 3; matrix products, arithmetic and copies ran while one was open for 1% -> 3% of each run, Pallas kernels for 0% -> 0%
where the time goes in v1:
time: 120 us
  waiting for transfers between devices  36.9 us (31%)
  blocking collectives  29.1 us (24%)
  starting transfers between devices  15.1 us (13%)
  between operations  14.2 us (12%)
  matrix products  9.75 us (8%)
  other arithmetic  7.86 us (7%)
  local copies, waits for them, and re-layouts  7.03 us (6%)
    all_gather x1, blocking collectives, on_device(): lax.all_gather(lat_filter, 'col', axis=1, tiled=True)  29.1 us
    reduce_scatter x1, waiting for transfers between devices, on_device(): return lax.psum_scatter(terms, 'mem', scatter_dimension=0, tiled=True)  21.8 us
    all_to_all x1, waiting for transfers between devices, on_device(): lax.all_to_all(filtered, 'col', split_axis=1, concat_axis=0, tiled=True)  14.7 us
    all_to_all x1, starting transfers between devices, on_device(): lax.all_to_all(filtered, 'col', split_axis=1, concat_axis=0, tiled=True)  6.16 us
    all_to_all x1, starting transfers between devices, on_device(): lax.all_to_all(schur, 'col', split_axis=0, concat_axis=1, tiled=True)  5.94 us
    dot_general x1, matrix products, on_device(): jnp.einsum('sab,lsbi->lsai', lax.all_gather(lat_filter, 'col', axis=1, ti...  4.7 us
    unnamed x1, other arithmetic  4.37 us
    another operation x1, local copies, waits for them, and re-layouts  3.98 us
  transfers between devices with their start and end apart: 4, of which 3 were waited for; matrix products, arithmetic and copies ran while one was open for 3% of the time, Pallas kernels for 0%

profile of v1, /device:TPU:0, one launch (start us, length us, event | category | flops | bytes accessed | tf_op | source)
XLA Modules:
  0.0 119.9 jit_solution(4190235565283901568)
XLA Ops:
  6.5 3.0 %collective-permute-start = (bf16[3,384,768]{2,1,0:T(8,128)(2,1)}, bf16[3,384,768]{2,1,0:T(8,128)(2,1)}, u32[]{:S(2)}, u32[]{:S(2)}) collective-permute-start(bf16[3,384,768]{2,1,0:T(8,128)(2,1)} %param.10), channel_id=1, source_target_pairs={{0,16},{16,0},{1,17},{17,1},{2,18},{18,2},{3,19},{19,3},{4,20},{20... | collective-permute-start | bytes 5308424 | tf_op jit(solution)/shard_map/ppermute | solution.py:12
  9.5 2.3 %fusion.7 = bf16[16,24,768]{2,1,0:T(8,128)(2,1)} fusion(f32[16,24,768]{2,1,0:T(8,128)} %param.7, bf16[1,16,24,768]{3,2,1,0:T(8,128)(2,1)} %param.6), kind=kLoop, calls=%fused_computation.15 | loop fusion | flops 884736 | bytes 2359296 | tf_op jit(solution)/shard_map/convert_element_type | solution.py:24
  11.9 5.9 %all-to-all-start = ((bf16[16,24,768]{2,1,0:T(8,128)(2,1)}), bf16[16,24,768]{2,1,0:T(8,128)(2,1)S(1)}, u32[]{:S(2)}, u32[]{:S(2)}) async-start(bf16[16,24,768]{2,1,0:T(8,128)(2,1)} %fusion.7), calls=%async_computation | async-start | bytes 1179648 | tf_op jit(solution)/shard_map/all_to_all | solution.py:25
  17.8 29.1 %all_gather.3 = bf16[3,384,384]{2,1,0:T(8,128)(2,1)S(1)} all-gather(bf16[3,24,384]{2,1,0:T(8,128)(2,1)S(1)} %copy-done.2), channel_id=1, replica_groups=mesh['mem'=2,'col'=16] {'col'}, dimensions={1}, use_global_device_ids=true | all-gather | bytes 940032 | tf_op jit(solution)/shard_map/all_gather | solution.py:37
  46.9 1.1 convolution_bitcast_fusion.1
  48.0 0.4 collective-permute-done
  48.5 2.6 %convolution_bitcast_fusion.2 = bf16[1,3,384,384]{2,3,1,0:T(8,128)(2,1)S(1)} fusion(bf16[384,768,1]{1,0,2:T(8,128)(2,1)S(1)} %bitcast.65, bf16[3,384,768]{2,1,0:T(8,128)(2,1)} %collective-permute-done), kind=kOutput, calls=%fused_computation.11 | convolution fusion | flops 679477248 | bytes 3244032 | tf_op jit(solution)/shard_map/laj,sij->lsai/dot_general | solution.py:30
  51.0 4.7 %convolution_bitcast_fusion = bf16[3,384,768]{1,2,0:T(8,128)(2,1)} fusion(bf16[3,384,384]{2,1,0:T(8,128)(2,1)S(1)} %all_gather.3, s32[]{:T(128)S(6)} %select_n.14, bf16[1,3,384,384]{2,3,1,0:T(8,128)(2,1)S(1)} %convolution_bitcast_fusion.2, bf16[1,3,384,384]{2,3,1,0:T(8,128)(2,1)S(1)} %convolution_bitcast_fusion.1), kind=kOutput, calls=%fused_computation.8 | convolution fusion | flops 686555136 | bytes 4423684 | tf_op jit(solution)/shard_map/sab,lsbi->lsai/dot_general | solution.py:35
  55.7 4.0 %copy.8 = bf16[3,384,768]{2,0,1:T(4,128)(2,1)S(1)} copy(bf16[3,384,768]{1,2,0:T(8,128)(2,1)} %convolution_bitcast_fusion) | data formatting | bytes 3538944 | tf_op jit(solution)/shard_map/reshape.9
  59.7 1.4 %fusion.14 = bf16[1,384,768]{2,0,1:T(2,128)(2,1)S(1)} fusion(bf16[3,384,768]{2,0,1:T(4,128)(2,1)S(1)} %copy.8, f32[3]{0:T(128)S(1)} %copy-done), kind=kOutput, calls=%fused_computation.23 | convolution fusion | flops 1769472 | bytes 2359308 | tf_op jit(solution)/shard_map/s,lsai->lai/dot_general | solution.py:41
  61.1 0.1 copy.15
  61.2 0.9 copy.16
  62.1 0.5 broadcast
  62.6 4.4 %reduce = bf16[384,768]{1,0:T(8,128)(2,1)S(1)} reduce(bf16[384,1,768]{2,1,0:T(2,128)(2,1)S(1)} %bitcast.62, bf16[]{:T(256)} %broadcast), dimensions={1}, to_apply=%bitcast.59.reduce_sub_computation | reduce | bytes 1179650
  67.0 1.0 reshape.35
  68.0 6.2 %all-to-all-start.1 = ((bf16[16,2,9216]{2,1,0:T(2,128)(2,1)}), bf16[16,2,9216]{2,1,0:T(2,128)(2,1)S(1)}, u32[]{:S(2)}, u32[]{:S(2)}) async-start(bf16[16,2,9216]{2,1,0:T(2,128)(2,1)} %reshape.35), calls=%async_computation.1 | async-start | bytes 1179648 | tf_op jit(solution)/shard_map/all_to_all | solution.py:42
  74.1 0.0 reduce-scatter.2.cloned.1.call-start
  74.8 0.0 copy-start.1
  74.8 14.7 %all-to-all-done.1 = bf16[16,2,9216]{2,1,0:T(2,128)(2,1)S(1)} async-done(((bf16[16,2,9216]{2,1,0:T(2,128)(2,1)}), bf16[16,2,9216]{2,1,0:T(2,128)(2,1)S(1)}, u32[]{:S(2)}, u32[]{:S(2)}) %all-to-all-start.1) | async-done | bytes 589856 | tf_op jit(solution)/shard_map/all_to_all | solution.py:42
  89.5 0.5 reshape.36
  90.0 0.1 copy.10
  90.1 1.1 fusion.6
  91.2 0.0 reduce-scatter.2.cloned.1.call-update
  91.3 21.8 %reduce-scatter.2.cloned.1.call-done = f32[8,24,768]{2,1,0:T(8,128)} async-done(((f32[16,24,768]{2,1,0:T(8,128)}), f32[8,24,768]{2,1,0:T(8,128)}) %reduce-scatter.2.cloned.1.call-update) | async-done | bytes 589840 | tf_op jit(solution)/shard_map/reduce_scatter | solution.py:44
  (8 shorter events, 0.0 us)
Async XLA Ops:
  6.5 53.2 %copy-start = (f32[3]{0:T(128)S(1)}, f32[3]{0:T(128)}, u32[]{:S(2)}) copy-start(f32[3]{0:T(128)} %param.9) | copy-start | bytes 40
  6.5 40.4 %copy-start.3 = (bf16[3,384,768]{2,1,0:T(8,128)(2,1)S(1)}, bf16[3,384,768]{2,1,0:T(8,128)(2,1)}, u32[]{:S(2)}) copy-start(bf16[3,384,768]{2,1,0:T(8,128)(2,1)} %param.10) | copy-start | bytes 5308420
  6.5 11.3 %copy-start.2 = (bf16[3,24,384]{2,1,0:T(8,128)(2,1)S(1)}, bf16[3,24,384]{2,1,0:T(8,128)(2,1)}, u32[]{:S(2)}) copy-start(bf16[3,24,384]{2,1,0:T(8,128)(2,1)} %param.11) | copy-start | bytes 165892
  6.5 41.9 %collective-permute-start = (bf16[3,384,768]{2,1,0:T(8,128)(2,1)}, bf16[3,384,768]{2,1,0:T(8,128)(2,1)}, u32[]{:S(2)}, u32[]{:S(2)}) collective-permute-start(bf16[3,384,768]{2,1,0:T(8,128)(2,1)} %param.10), channel_id=1, source_target_pairs={{0,16},{16,0},{1,17},{17,1},{2,18},{18,2},{3,19},{19,3},{4,20},{20... | collective-permute-start | bytes 5308424 | tf_op jit(solution)/shard_map/ppermute | solution.py:12
  11.9 35.1 %all-to-all-start = ((bf16[16,24,768]{2,1,0:T(8,128)(2,1)}), bf16[16,24,768]{2,1,0:T(8,128)(2,1)S(1)}, u32[]{:S(2)}, u32[]{:S(2)}) async-start(bf16[16,24,768]{2,1,0:T(8,128)(2,1)} %fusion.7), calls=%async_computation | async-start | bytes 1179648 | tf_op jit(solution)/shard_map/all_to_all | solution.py:25
  68.0 21.5 %all-to-all-start.1 = ((bf16[16,2,9216]{2,1,0:T(2,128)(2,1)}), bf16[16,2,9216]{2,1,0:T(2,128)(2,1)S(1)}, u32[]{:S(2)}, u32[]{:S(2)}) async-start(bf16[16,2,9216]{2,1,0:T(2,128)(2,1)} %reshape.35), calls=%async_computation.1 | async-start | bytes 1179648 | tf_op jit(solution)/shard_map/all_to_all | solution.py:42
  74.1 38.9 %reduce-scatter.2.cloned.1.call-start = ((), (), s32[]{:S(2)}) async-start(), calls=%async_computation.3 | async-start | bytes 1769472 | tf_op jit(solution)/shard_map/reduce_scatter | solution.py:44
  74.8 15.3 %copy-start.1 = (bf16[1,16,24,768]{3,2,1,0:T(8,128)(2,1)S(1)}, bf16[1,16,24,768]{3,2,1,0:T(8,128)(2,1)}, u32[]{:S(2)}) copy-start(bf16[1,16,24,768]{3,2,1,0:T(8,128)(2,1)} %param.6) | copy-start | bytes 1769476
Sparse Core Ops, SparseCore 0:
  91.4 21.6 reduce-scatter.1
